TPU v7x, 32 devices: a whole 2x2x4 slice. The times are simulated.
32 devices in a mesh: dp: 16 (over z, y, x), feat: 2 (over core).
Axes of the slice: x: 2, y: 2, z: 4, core: 2. Of those that a mesh axis runs over, the one named last changes fastest.
Arguments:
- embeddings: bfloat16 [81920, 2048], P('dp', 'feat'), may hold values from -80 to 80
- slot_image: int32 [81920], P('dp'), may hold values from 0 to 8191, as said below
- slot_view: int32 [81920], P('dp'), may hold values from 0 to 10, as said below
- pair_table: int32 [2, 2], replicated, may hold values from 0 to 9, as said below
Outputs:
- correlation: float32 [2, 2048, 2048], P(None, 'feat', 'dp')
Inputs may be any that keep to these rules, and one draw needn't show every extreme that they name: `slot_image`: image ids of dp index d run from d * 512 to (d + 1) * 512 - 1. Each image has views 0 and 1 and local views 2 to 1 + k with k from 1 to 8; the first image of every dp index has all 10 views; every (image, view) stands in one slot at most; empty slots name an image of their own dp index. `slot_view`: empty slots carry view 10 and come after the used slots of their dp index; the last dp index fills all its slots. `pair_table`: each pair's first view is global (0 or 1) and its second view differs from it.
All inputs are finite; a program needn't handle non-finite values.
Results may differ from a plain program's by a relative error of at most 0.00035.
Values may be sent and summed in bfloat16 or wider, within the bound.
No kernel may reach another device: no remote copies, remote signals or barrier semaphores. Data moves between devices by JAX's collectives and lax.ppermute only.
A program may use at most 64 MiB of HBM per device.

v0:
```python
import jax
import jax.numpy as jnp
from jax import lax
from jax.experimental import pallas as pl
from jax.experimental.pallas import tpu as pltpu
from jax.sharding import PartitionSpec as P

VIEWS = 10
PAIRS = 2
EPS = 1e-05
CHUNKS = 2
STEPS = 10
UNIT = 16384.0


def swap(value, axis, mask):
    size = lax.axis_size(axis)
    return lax.ppermute(value, axis, [(k, k ^ mask) for k in range(size)])


def bits_of(size):
    return size.bit_length() - 1


def select_kernel(image_ref, view_ref, pair_ref, emb_ref, *refs):
    firsts = (refs[:CHUNKS], refs[CHUNKS : 2 * CHUNKS])
    kept, away, stats = (refs[2 * CHUNKS + k : 2 * CHUNKS + k + 2] for k in (0, 2, 4))
    raw, wide, held, turned, slots, sem, slot_sem = refs[2 * CHUNKS + 6 :]
    rows, width = raw.shape
    pieces = width // 128
    images = firsts[0][0].shape[0]
    step = rows // STEPS

    def fetch(k):
        part = pl.ds(k * step, step)
        return pltpu.make_async_copy(emb_ref.at[part, :], raw.at[part, :], sem.at[k])

    for k in range(STEPS):
        fetch(k).start()
    image = image_ref[...] - lax.axis_index("dp") * images
    view = view_ref[...]
    groups = images // 16
    upper = lax.broadcasted_iota(jnp.int32, (groups, rows), 0)
    hits = jnp.where(upper == jnp.right_shift(image, 4), 1.0, 0.0).astype(jnp.bfloat16)
    lower = jnp.bitwise_and(image, 15) * 16 + view
    line = lax.broadcasted_iota(jnp.int32, (96, 1), 0)
    place = lax.broadcasted_iota(jnp.int32, (32, rows), 1)
    values = jnp.concatenate(
        [jnp.right_shift(place, 6), jnp.bitwise_and(place, 63), jnp.ones_like(place)], 0
    ).astype(jnp.float32)
    found = []
    for role in range(2):
        wanted = jnp.bitwise_and(line, 15) * 16 + jnp.where(
            jnp.bitwise_and(line, 16) == 0, pair_ref[0, role], pair_ref[1, role]
        )
        marks = jnp.where(wanted == lower, values, 0.0).astype(jnp.bfloat16)
        marks = jnp.concatenate([marks, jnp.zeros((32, rows), jnp.bfloat16)], 0)
        found.append(
            lax.dot_general(
                hits, marks, (((1,), (1,)), ((), ())), preferred_element_type=jnp.float32
            )
        )
    both = pltpu.roll(found[0], 64, 1) * pltpu.roll(found[1], 64, 1) > 0.5
    for ref in stats:
        ref[...] = jnp.zeros_like(ref)
    lanes = lax.broadcasted_iota(jnp.int32, (groups, 128), 1)
    for p in range(2):
        mine = both & (lanes >= 16 * p) & (lanes < 16 * p + 16)
        amount = jnp.sum(jnp.sum(mine.astype(jnp.float32), axis=0, keepdims=True), axis=1, keepdims=True)
        stats[p][0:1, width : width + 128] = jnp.broadcast_to(amount, (1, 128))
    for role in range(2):
        slot = jnp.minimum(found[role] * 64.0 + pltpu.roll(found[role], 96, 1), float(rows))
        turned[role * groups : (role + 1) * groups, :] = jnp.where(both, slot, float(rows)).astype(
            jnp.int32
        )
    to_scalar = pltpu.make_async_copy(turned, slots, slot_sem)
    to_scalar.start()
    wide[pl.ds(rows * pieces, pieces), :] = jnp.zeros((pieces, 128), jnp.float32)
    for k in range(STEPS):
        fetch(k).wait()

        def widen(t, carry):
            start = pl.multiple_of(k * step + t * 32, 32)
            for c in range(pieces):
                wide[pl.ds(start * pieces + c, 32, stride=pieces), :] = raw[
                    pl.ds(start, 32), c * 128 : (c + 1) * 128
                ].astype(jnp.float32)
            return carry

        lax.fori_loop(0, step // 32, widen, 0)
    to_scalar.wait()

    def gather(t, carry):
        for u in range(16):
            n = t * 16 + u
            for k in range(4):
                slot = slots[(k % 2) * groups + t, (k // 2) * 16 + u]
                held[pl.ds(pl.multiple_of((k * images + n) * pieces, pieces), pieces), :] = wide[
                    pl.ds(pl.multiple_of(slot * pieces, pieces), pieces), :
                ]
        return carry

    lax.fori_loop(0, groups, gather, 0)
    me = lax.axis_index("dp")
    mine = [jnp.bitwise_and(jnp.right_shift(me, bit), 1) for bit in range(2)]
    span = width // CHUNKS // 128
    for k in range(4):
        p, line = k // 2, 2 * (k % 2)
        for m in range(pieces):
            if k % 2:
                near, over, rest = m // 4, (m // 2) % 2, m % 2
                near_value = mine[p] if near else 1 - mine[p]
                over_value = mine[1 - p] if over else 1 - mine[1 - p]
                c = rest * 4 + near_value * (1 << p) + over_value * (2 >> p)
                out = (kept if near else away)[p]
                lane = (m % 4) * 128
            else:
                c, out, lane = m, firsts[p][m // span], (m % span) * 128

            def emit(t, carry):
                sums, squares = carry
                start = pl.multiple_of(t * 128, 128)
                value = held[pl.ds((k * images + start) * pieces + c, 128, stride=pieces), :]
                out[pl.ds(start, 128), lane : lane + 128] = value.astype(jnp.bfloat16)
                value = value.reshape(16, 8, 128)
                return sums + value.sum(0), squares + (value * value).sum(0)

            zero = jnp.zeros((8, 128), jnp.float32)
            sums, squares = lax.fori_loop(0, images // 128, emit, (zero, zero))
            at = pl.ds(pl.multiple_of(c * 128, 128), 128)
            stats[p][line : line + 1, at] = jnp.sum(sums, axis=0, keepdims=True)
            stats[p][line + 1 : line + 2, at] = jnp.sum(squares, axis=0, keepdims=True)


def select_all(embeddings, slot_image, slot_view, pair_table, images):
    rows, width = embeddings.shape
    pieces = width // 128
    vmem = pl.BlockSpec(memory_space=pltpu.VMEM)
    return pl.pallas_call(
        select_kernel,
        out_shape=[jax.ShapeDtypeStruct((images, width // CHUNKS), jnp.bfloat16)] * (2 * CHUNKS)
        + [jax.ShapeDtypeStruct((images, width // 2), jnp.bfloat16)] * 4
        + [jax.ShapeDtypeStruct((8, width + 128), jnp.float32)] * 2,
        in_specs=[vmem, vmem, pl.BlockSpec(memory_space=pltpu.SMEM), pl.BlockSpec(memory_space=pl.ANY)],
        out_specs=[vmem] * (2 * CHUNKS + 6),
        scratch_shapes=[
            pltpu.VMEM((rows, width), jnp.bfloat16),
            pltpu.VMEM(((rows + 1) * pieces, 128), jnp.float32),
            pltpu.VMEM((4 * pieces * images, 128), jnp.float32),
            pltpu.VMEM((images // 8, 128), jnp.int32),
            pltpu.SMEM((images // 8, 128), jnp.int32),
            pltpu.SemaphoreType.DMA((STEPS,)),
            pltpu.SemaphoreType.DMA,
        ],
        compiler_params=pltpu.CompilerParams(vmem_limit_bytes=60 << 20),
        name="select",
    )(slot_image.reshape(1, -1), slot_view.reshape(1, -1), pair_table, embeddings)


def turn_kernel(*refs):
    for p in range(PAIRS):
        kept, kept_other, come, come_other = refs[4 * p : 4 * p + 4]
        out = refs[4 * PAIRS + p]
        images, half = kept.shape[0], kept.shape[1] // 2
        for column, sources in enumerate(((kept, kept_other), (come, come_other))):
            for line in range(2):
                for s in range(2):
                    row = (2 * line + s) * half
                    out[row : row + half, column * images : (column + 1) * images] = jnp.transpose(
                        sources[s][:, line * half : (line + 1) * half]
                    )


def turn(operands):
    images, half = operands[0].shape
    vmem = pl.BlockSpec(memory_space=pltpu.VMEM)
    return pl.pallas_call(
        turn_kernel,
        out_shape=[jax.ShapeDtypeStruct((2 * half, 2 * images), jnp.bfloat16)] * PAIRS,
        in_specs=[vmem] * (4 * PAIRS),
        out_specs=[vmem] * PAIRS,
        cost_estimate=pl.CostEstimate(flops=0, bytes_accessed=16 * half * images, transcendentals=0),
        compiler_params=pltpu.CompilerParams(vmem_limit_bytes=32 << 20),
        name="turn",
    )(*operands)


def moment_kernel(total_ref, group0, group1, rows_ref, lines_ref, work):
    width = rows_ref.shape[1]
    me = lax.axis_index("dp")
    mine = [jnp.bitwise_and(jnp.right_shift(me, bit), 1) for bit in range(2)]
    rows_ref[...] = jnp.zeros_like(rows_ref)
    lines_ref[...] = jnp.zeros_like(lines_ref)
    for p, group in enumerate((group0, group1)):
        total = total_ref[8 * p : 8 * p + 8, :]
        count = total[0:1, width : width + 1]
        amount = group[0:1, width : width + 1]
        means, roots = [], []
        for role in range(2):
            mean = total[2 * role : 2 * role + 1, :width] / count
            square = total[2 * role + 1 : 2 * role + 2, :width] / count
            means.append(mean)
            roots.append(jnp.sqrt(square - mean * mean + EPS))
        rows_ref[8 * p : 8 * p + 1, :] = means[0]
        rows_ref[8 * p + 1 : 8 * p + 2, :] = group[0:1, :width] - amount * means[0]
        rows_ref[8 * p + 2 : 8 * p + 3, :] = UNIT / (count * roots[0])
        work[0:1, :] = group[2:3, :width]
        work[1:2, :] = means[1]
        work[2:3, :] = 1.0 / roots[1]
        for m in range(4):
            over_value = mine[1 - p] if m // 2 else 1 - mine[1 - p]
            c = (m % 2) * 4 + mine[p] * (1 << p) + over_value * (2 >> p)
            lines_ref[8 * p : 8 * p + 3, m * 128 : (m + 1) * 128] = work[
                0:3, pl.ds(pl.multiple_of(c * 128, 128), 128)
            ]


def moments(total, groups, width):
    vmem = pl.BlockSpec(memory_space=pltpu.VMEM)
    return pl.pallas_call(
        moment_kernel,
        out_shape=[
            jax.ShapeDtypeStruct((8 * PAIRS, width), jnp.float32),
            jax.ShapeDtypeStruct((8 * PAIRS, width // 2), jnp.float32),
        ],
        in_specs=[vmem] * 3,
        out_specs=[vmem] * 2,
        scratch_shapes=[pltpu.VMEM((8, width), jnp.float32)],
        cost_estimate=pl.CostEstimate(flops=0, bytes_accessed=400 * width, transcendentals=0),
        name="moments",
    )(total, *groups)


def product_kernel(turned0, turned1, near0, far0, near1, far1, rows_ref, lines, lines_other, *outs):
    go, stay = outs[:PAIRS], outs[PAIRS:]
    for p, (turned, near, far) in enumerate(((turned0, near0, far0), (turned1, near1, far1))):
        depth = near.shape[0]
        half = lines.shape[1] // 2
        own, other = lines[8 * p : 8 * p + 8, :], lines_other[8 * p : 8 * p + 8, :]
        mean = rows_ref[8 * p : 8 * p + 1, :]
        shift = rows_ref[8 * p + 1 : 8 * p + 2, :]
        rate = rows_ref[8 * p + 2 : 8 * p + 3, :]
        for part in range(4):
            side, s = part // 2, part % 2
            rows = slice(part * half, (part + 1) * half)
            value = jnp.dot(turned[rows, :depth], near[...], preferred_element_type=jnp.float32)
            value += jnp.dot(turned[rows, depth:], far[...], preferred_element_type=jnp.float32)
            column = jnp.transpose((other if s else own)[:, side * half : (side + 1) * half])
            value = value - column[:, 0:1] * mean - column[:, 1:2] * shift
            value = value * (column[:, 2:3] * rate)
            if side == 0:
                value = jnp.clip(value, -60000.0, 60000.0)
            (stay if side else go)[p][s * half : (s + 1) * half, :] = value


def product(turned, near, far, rows, lines, lines_other, c):
    vmem = pl.BlockSpec(memory_space=pltpu.VMEM)
    depth, chunk = near[0].shape
    half = turned[0].shape[0] // 2
    out = jax.ShapeDtypeStruct((half, chunk), jnp.float32)
    return pl.pallas_call(
        product_kernel,
        grid=(1,),
        out_shape=[out] * (2 * PAIRS),
        in_specs=[vmem] * 6 + [pl.BlockSpec((8 * PAIRS, chunk), lambda g: (0, c))] + [vmem] * 2,
        out_specs=[vmem] * (2 * PAIRS),
        cost_estimate=pl.CostEstimate(
            flops=2 * PAIRS * 4 * half * depth * chunk, bytes_accessed=16 * half * chunk, transcendentals=0
        ),
        compiler_params=pltpu.CompilerParams(vmem_limit_bytes=32 << 20),
        name="product",
    )(*turned, near[0], far[0], near[1], far[1], rows, lines, lines_other)


def fast(embeddings, slot_image, slot_view, pair_table, images):
    width = embeddings.shape[1]
    me, core = lax.axis_index("dp"), lax.axis_index("feat")
    mine = [(me >> bit) & 1 for bit in range(4)]
    block = 128
    chosen = select_all(embeddings, slot_image, slot_view, pair_table, images)
    firsts = (chosen[:CHUNKS], chosen[CHUNKS : 2 * CHUNKS])
    kept, away, stats = (chosen[2 * CHUNKS + k : 2 * CHUNKS + k + 2] for k in (0, 2, 4))
    near_bit, over_bit = (1, 2), (2, 1)
    groups = [stats[p] + swap(stats[p], "dp", near_bit[p]) for p in range(PAIRS)]
    come = [swap(away[p], "dp", near_bit[p]) for p in range(PAIRS)]
    kept_other = [swap(kept[p], "feat", 1) for p in range(PAIRS)]
    total = jnp.concatenate(
        [groups[p] + swap(groups[p], "dp", over_bit[p]) for p in range(PAIRS)], 0
    )
    far = [[swap(firsts[p][c], "dp", near_bit[p]) for c in range(CHUNKS)] for p in range(PAIRS)]
    total = total + swap(total, "dp", 4)
    total = total + swap(total, "dp", 8)
    rows, lines = moments(total, groups, width)
    lines_other = swap(lines, "feat", 1)
    come_other = [swap(come[p], "feat", 1) for p in range(PAIRS)]
    turned = turn([v for p in range(PAIRS) for v in (kept[p], kept_other[p], come[p], come_other[p])])
    finals = []
    for c in range(CHUNKS):
        values = product(
            turned,
            [firsts[p][c] for p in range(PAIRS)],
            [far[p][c] for p in range(PAIRS)],
            rows,
            lines,
            lines_other,
            c,
        )
        chunk = width // CHUNKS
        shape = (2, 2, block, chunk)
        sent = [
            swap(values[p].astype(jnp.float16), "dp", over_bit[p]).reshape(shape)
            for p in range(PAIRS)
        ]
        stay = [values[PAIRS + p].reshape(shape) for p in range(PAIRS)]

        def pick(value, at, axis):
            return lax.dynamic_index_in_dim(value, at, axis, keepdims=False)

        def merge(own, other, at, axis):
            return pick(own, at, axis) + pick(other, at, axis).astype(jnp.float32)

        go = jnp.stack([merge(stay[p], sent[p], 1 - mine[2], 1) for p in range(PAIRS)])
        go = swap(jnp.clip(go, -60000.0, 60000.0).astype(jnp.float16), "dp", 4)
        stay = jnp.stack([merge(stay[p], sent[p], mine[2], 1) for p in range(PAIRS)])
        keep_at = mine[3] ^ core
        last = jnp.clip(merge(stay, go, 1 - keep_at, 1), -60000.0, 60000.0).astype(jnp.float16)
        last = swap(last, "dp", 8)
        finals.append(merge(stay, go, keep_at, 1) + last.astype(jnp.float32))
    return jnp.swapaxes(jnp.concatenate(finals, 2), 1, 2) * (1.0 / UNIT)


def select_plain(embeddings, slot_image, slot_view, pair_table, images):
    width = embeddings.shape[1]
    local_image = slot_image - lax.axis_index("dp") * images
    image_grid = jnp.arange(images, dtype=jnp.int32)[:, None]
    rows, stats = [], []
    for p in range(PAIRS):
        marks = [
            (local_image[None, :] == image_grid) & (slot_view[None, :] == pair_table[p, role])
            for role in range(2)
        ]
        present = jnp.any(marks[0], axis=1) & jnp.any(marks[1], axis=1)
        lines = []
        for mark in marks:
            taken = jnp.dot(
                (mark & present[:, None]).astype(jnp.bfloat16),
                embeddings,
                preferred_element_type=jnp.float32,
            )
            rows.append(taken.astype(jnp.bfloat16))
            lines += [jnp.sum(taken, axis=0), jnp.sum(taken * taken, axis=0)]
        table = jnp.pad(jnp.stack(lines), ((0, 4), (0, 128)))
        amount = jnp.sum(present.astype(jnp.float32))
        stats.append(table.at[0, width:].set(amount))
    return (*rows, *stats)


def local(embeddings, slot_image, slot_view, pair_table):
    images = embeddings.shape[0] // VIEWS
    rows, width = embeddings.shape
    dp, feat = lax.axis_size("dp"), lax.axis_size("feat")
    me, core = lax.axis_index("dp"), lax.axis_index("feat")
    if (dp, feat, width) == (16, 2, 1024) and images % 128 == 0 and rows % (32 * STEPS) == 0:
        return fast(embeddings, slot_image, slot_view, pair_table, images)
    chosen = select_plain(embeddings, slot_image, slot_view, pair_table, images)
    block = width * feat // dp
    low, high = bits_of(width // block), bits_of(feat)
    mine = [(me >> bit) & 1 for bit in range(low + high)]
    chunk = width // CHUNKS
    orders = []
    for p in range(PAIRS):
        order = list(range(low + high))
        if p % 2:
            order[:2] = order[1::-1]
        orders.append(order)
    rest_bits = list(range(2, low))[::-1]
    shape = (2,) * high + (2,) * len(rest_bits) + (block,)

    def columns(rows, bits, values):
        parts = []
        for code in range(1 << len(rest_bits)):
            start = sum(value << bit for bit, value in zip(bits, values))
            for place, bit in enumerate(rest_bits[::-1]):
                start = start + (((code >> place) & 1) << bit)
            parts.append(lax.dynamic_slice_in_dim(rows, start * block, block, 1))
        return parts

    def halves(rows, order, near_value):
        far = columns(rows, order[:2], (near_value, 1 - mine[order[1]]))
        return jnp.concatenate(far + columns(rows, order[:2], (near_value, mine[order[1]])), 1)

    def across(value):
        return jnp.stack([value] + [swap(value, "feat", s) for s in range(1, feat)], 0)

    firsts = [chosen[0], chosen[2]]
    seconds = [chosen[1], chosen[3]]
    stats = list(chosen[4:])
    kept = [halves(seconds[p], orders[p], mine[orders[p][0]]) for p in range(PAIRS)]
    away = [halves(seconds[p], orders[p], 1 - mine[orders[p][0]]) for p in range(PAIRS)]
    group = [stats[p] + swap(stats[p], "dp", 1 << orders[p][0]) for p in range(PAIRS)]
    come = [swap(away[p], "dp", 1 << orders[p][0]) for p in range(PAIRS)]
    totals = list(group)
    for step in range(1, low + high):
        totals = [totals[p] + swap(totals[p], "dp", 1 << orders[p][step]) for p in range(PAIRS)]
    pieces = [[firsts[p][:, c * chunk : (c + 1) * chunk] for c in range(CHUNKS)] for p in range(PAIRS)]
    far = [[None] * CHUNKS for _ in range(PAIRS)]
    for c in range(CHUNKS):
        for p in range(PAIRS):
            far[p][c] = swap(pieces[p][c], "dp", 1 << orders[p][0])
    kept_all = [across(kept[p]) for p in range(PAIRS)]
    come_all = [across(come[p]) for p in range(PAIRS)]
    half = kept_all[0].shape[2] // 2

    def multiply(left, right):
        return lax.dot_general(
            left, right, (((1,), (0,)), ((), ())), preferred_element_type=jnp.float32
        )

    vectors = []
    for p in range(PAIRS):
        count, amount = totals[p][0, width], group[p][0, width]
        mean = totals[p][0:4:2, :width] / count
        root = jnp.sqrt(totals[p][1:4:2, :width] / count - mean * mean + EPS)
        first_rate = UNIT / (count * root[0])
        first_shift = group[p][0, :width] - amount * mean[0]
        lines = jnp.stack([group[p][2, :width], mean[1], 1.0 / root[1]])
        lines = halves(lines, orders[p], mine[orders[p][0]])
        lines = across(lines)
        vectors.append((mean[0], first_shift, first_rate, lines))

    def product(p, c, side):
        at = slice(side * half, (side + 1) * half)
        value = multiply(kept_all[p][:, :, at], pieces[p][c]) + multiply(
            come_all[p][:, :, at], far[p][c]
        )
        mean, shift, rate, lines = vectors[p]
        span = slice(c * chunk, (c + 1) * chunk)
        lines = lines[:, :, at, None]
        value = value - lines[:, 0] * mean[span] - lines[:, 1] * shift[span]
        return (value * (lines[:, 2] * rate[span])).reshape(shape + (chunk,))

    def narrow(value):
        return jnp.clip(value, -60000.0, 60000.0).astype(jnp.float16)

    stay = [[None] * CHUNKS for _ in range(PAIRS)]
    for c in range(CHUNKS):
        for p in range(PAIRS):
            sent = swap(narrow(product(p, c, 0)), "dp", 1 << orders[p][1])
            stay[p][c] = product(p, c, 1) + sent.astype(jnp.float32)
    axes = list(range(low, low + high))[::-1] + rest_bits
    for bit in range(2, low + high):
        axis = axes.index(bit)
        axes.remove(bit)
        keep_at = mine[bit] ^ ((core >> (bit - low)) & 1) if bit >= low else mine[bit]
        for c in range(CHUNKS):
            for p in range(PAIRS):
                go = lax.dynamic_index_in_dim(stay[p][c], 1 - keep_at, axis, keepdims=False)
                sent = swap(narrow(go), "dp", 1 << bit)
                own = lax.dynamic_index_in_dim(stay[p][c], keep_at, axis, keepdims=False)
                stay[p][c] = own + sent.astype(jnp.float32)
    return jnp.stack(
        [jnp.concatenate([stay[p][c].T for c in range(CHUNKS)], 0) for p in range(PAIRS)]
    ) * (1.0 / UNIT)


def solution(mesh):
    in_specs = (P("dp", "feat"), P("dp"), P("dp"), P())
    out_specs = P(None, "feat", "dp")
    step = jax.shard_map(local, mesh=mesh, in_specs=in_specs, out_specs=out_specs, check_vma=False)
    if dict(mesh.shape) != {"dp": 16, "feat": 2}:
        return step
    return step
```

profile of v0, /device:TPU:0, one launch (start us, length us, event | category | flops | bytes accessed | tf_op | source)
XLA Modules:
  0.0 145.2 jit_solution(3010403786047506053)
XLA Ops:
  0.0 13.8 %select.1 = (bf16[512,512]{1,0:T(8,128)(2,1)}, bf16[512,512]{1,0:T(8,128)(2,1)}, bf16[512,512]{1,0:T(8,128)(2,1)}, bf16[512,512]{1,0:T(8,128)(2,1)}, bf16[512,51...) custom-call(s32[1,5120]{1,0:T(1,128)} %bitcast.44, ...), custom_call_target="tpu_custom_call" | custom-call | tf_op jit(solution)/shard_map/select/pallas_call | solution.py:139
  13.8 3.0 %collective-permute-start.1 = (bf16[512,512]{1,0:T(8,128)(2,1)}, bf16[512,512]{1,0:T(8,128)(2,1)S(1)}, u32[]{:S(2)}, u32[]{:S(2)}) collective-permute-start(bf16[512,512]{1,0:T(8,128)(2,1)} %get-tuple-element.28), channel_id=1, source_target_pairs={{0,2},{2,0},{4,6},{6,4},{8,10},{10,8},{12,14},{14,12},{16,18},{18,... | collective-permute-start | bytes 1572872 | tf_op jit(solution)/shard_map/ppermute | solution.py:18
  16.9 2.0 %collective-permute-start.10 = (f32[8,1152]{1,0:T(8,128)}, f32[8,1152]{1,0:T(8,128)S(1)}, u32[]{:S(2)}, u32[]{:S(2)}) collective-permute-start(f32[8,1152]{1,0:T(8,128)} %get-tuple-element.36), channel_id=1, source_target_pairs={{0,4},{2,6},{4,0},{6,2},{8,12},{10,14},{12,8},{14,10},{16,20},{18,... | collective-permute-start | bytes 110600 | tf_op jit(solution)/shard_map/ppermute | solution.py:18
  18.9 10.9 %collective-permute-done.8 = f32[8,1152]{1,0:T(8,128)S(1)} collective-permute-done((f32[8,1152]{1,0:T(8,128)}, f32[8,1152]{1,0:T(8,128)S(1)}, u32[]{:S(2)}, u32[]{:S(2)}) %collective-permute-start.8) | collective-permute-done | bytes 36896 | tf_op jit(solution)/shard_map/ppermute | solution.py:18
  30.5 1.8 %collective-permute-start.9 = (f32[8,1152]{1,0:T(8,128)S(1)}, f32[8,1152]{1,0:T(8,128)S(1)}, u32[]{:S(2)}, u32[]{:S(2)}) collective-permute-start(f32[8,1152]{1,0:T(8,128)S(1)} %add.184.group0), channel_id=1, source_target_pairs={{0,4},{2,6},{4,0},{6,2},{8,12},{10,14},{12,8},{14,10},{16,20},{18,... | collective-permute-start | bytes 110600 | tf_op jit(solution)/shard_map/ppermute | solution.py:18
  34.6 2.5 %collective-permute-done.11 = f32[8,1152]{1,0:T(8,128)S(1)} collective-permute-done((f32[8,1152]{1,0:T(8,128)S(1)}, f32[8,1152]{1,0:T(8,128)S(1)}, u32[]{:S(2)}, u32[]{:S(2)}) %collective-permute-start.11) | collective-permute-done | bytes 36896 | tf_op jit(solution)/shard_map/ppermute | solution.py:18
  39.7 1.8 %collective-permute-done.12 = f32[16,1152]{1,0:T(8,128)S(1)} collective-permute-done((f32[16,1152]{1,0:T(8,128)S(1)}, f32[16,1152]{1,0:T(8,128)S(1)}, u32[]{:S(2)}, u32[]{:S(2)}) %collective-permute-start.12) | collective-permute-done | bytes 73760 | tf_op jit(solution)/shard_map/ppermute | solution.py:18
  41.5 2.7 %collective-permute-start.13 = (f32[16,1152]{1,0:T(8,128)S(1)}, f32[16,1152]{1,0:T(8,128)S(1)}, u32[]{:S(2)}, u32[]{:S(2)}) collective-permute-start(f32[16,1152]{1,0:T(8,128)S(1)} %fusion.21), channel_id=1, source_target_pairs={{0,16},{2,18},{4,20},{6,22},{8,24},{10,26},{12,28},{14,30},{16,0},... | collective-permute-start | bytes 221192 | tf_op jit(solution)/shard_map/ppermute | solution.py:18
  44.1 6.1 %collective-permute-done.4.refs_6_ = bf16[512,512]{1,0:T(8,128)(2,1)S(1)} collective-permute-done((bf16[512,512]{1,0:T(8,128)(2,1)}, bf16[512,512]{1,0:T(8,128)(2,1)S(1)}, u32[]{:S(2)}, u32[]{:S(2)}) %collective-permute-start.4) | collective-permute-done | bytes 524320 | tf_op jit(solution)/shard_map/ppermute | solution.py:18
  60.1 5.3 %collective-permute-done.6.far0 = bf16[512,512]{1,0:T(8,128)(2,1)} collective-permute-done((bf16[512,512]{1,0:T(8,128)(2,1)}, bf16[512,512]{1,0:T(8,128)(2,1)}, u32[]{:S(2)}, u32[]{:S(2)}) %collective-permute-start.6) | collective-permute-done | bytes 524320 | tf_op jit(solution)/shard_map/ppermute | solution.py:18
  66.9 4.2 %product.2 = (f32[512,512]{1,0:T(8,128)S(1)}, f32[512,512]{1,0:T(8,128)S(1)}, f32[512,512]{1,0:T(8,128)S(1)}, f32[512,512]{1,0:T(8,128)S(1)}) custom-call(bf16[1024,1024]{1,0:T(8,128)(2,1)S(1)} %get-tuple-element.31.turned0, bf16[1024,1024]{1,0:T(8,128)(2,1)S(1)} %get-tuple-element.32.turned1, bf16[512,512]{1,0:T(8,128)(2,1)S(1)} %copy-done.8, ...), custom_call_target="tpu_custom_call" | custom-call | flops 2147483648 | bytes 4194304 | tf_op jit(solution)/shard_map/product/pallas_call | solution.py:261
  75.1 2.2 %copy.25 = f32[2,1,128,512]{2,3,0,1:T(8,128)} copy(f32[2,1,128,512]{3,2,1,0:T(8,128)} %get-tuple-element.72) | data formatting | bytes 1048576
  77.3 2.0 %copy.27 = f32[2,1,128,512]{2,3,0,1:T(8,128)} copy(f32[2,1,128,512]{3,2,1,0:T(8,128)} %get-tuple-element.51) | data formatting | bytes 1048576
  79.4 2.0 %copy.23 = f32[2,1,128,512]{2,3,0,1:T(8,128)} copy(f32[2,1,128,512]{3,2,1,0:T(8,128)} %get-tuple-element.52) | data formatting | bytes 1048576
  81.4 2.0 %copy.21 = f32[2,1,128,512]{2,3,0,1:T(8,128)} copy(f32[2,1,128,512]{3,2,1,0:T(8,128)} %get-tuple-element.71) | data formatting | bytes 1048576
  85.1 4.2 %product.3 = (f32[512,512]{1,0:T(8,128)S(1)}, f32[512,512]{1,0:T(8,128)S(1)}, f32[512,512]{1,0:T(8,128)S(1)}, f32[512,512]{1,0:T(8,128)S(1)}) custom-call(bf16[1024,1024]{1,0:T(8,128)(2,1)S(1)} %copy-done.3, bf16[1024,1024]{1,0:T(8,128)(2,1)S(1)} %copy-done.5, bf16[512,512]{1,0:T(8,128)(2,1)S(1)} %copy-done.6, ...), custom_call_target="tpu_custom_call" | custom-call | flops 2147483648 | bytes 4194304 | tf_op jit(solution)/shard_map/product/pallas_call | solution.py:261
  90.1 1.7 %collective-permute-start.21 = (f16[512,512]{1,0:T(8,128)(2,1)}, f16[512,512]{1,0:T(8,128)(2,1)}, u32[]{:S(2)}, u32[]{:S(2)}) collective-permute-start(f16[512,512]{1,0:T(8,128)(2,1)} %convert_element_type.152), channel_id=1, source_target_pairs={{0,4},{2,6},{4,0},{6,2},{8,12},{10,14},{12,8},{14,10},{16,20},{18,... | collective-permute-start | bytes 1572872 | tf_op jit(solution)/shard_map/ppermute | solution.py:18
  96.2 2.3 %constant_dynamic-slice_fusion.8 = (f16[2,1,128,512]{3,2,1,0:T(8,128)(2,1)}, f16[2,1,128,512]{3,2,1,0:T(8,128)(2,1)S(1)}, f16[2,1,128,512]{3,2,1,0:T(8,128)(2,1)}, f16[2,1,128,512]{3,2,1,0:T(8,128)(2,1)S(1)}) fusion(f16[2,2,128,512]{3,2,1,0:T(8,128)(2,1)} %bitcast.6, s32[]{:T(128)S(6)} %select_n.36, s32[]{:T(128)S(6)} %select_n.34, ...), kind=kLoop, calls=%fused_computation.49 | loop fusion | bytes 2097160 | tf_op jit(solution)/shard_map/jit(dynamic_index_in_dim)/dynamic_slice | solution.py:317
  102.4 2.3 %collective-permute-done.22 = f16[512,512]{1,0:T(8,128)(2,1)} collective-permute-done((f16[512,512]{1,0:T(8,128)(2,1)}, f16[512,512]{1,0:T(8,128)(2,1)}, u32[]{:S(2)}, u32[]{:S(2)}) %collective-permute-start.22) | collective-permute-done | bytes 524320 | tf_op jit(solution)/shard_map/ppermute | solution.py:18
  104.7 2.2 %constant_dynamic-slice_fusion.1 = (f16[2,1,128,512]{3,2,1,0:T(8,128)(2,1)S(1)}, f16[2,1,128,512]{3,2,1,0:T(8,128)(2,1)}, f16[2,1,128,512]{3,2,1,0:T(8,128)(2,1)}, f16[2,1,128,512]{3,2,1,0:T(8,128)(2,1)S(1)}) fusion(f16[2,2,128,512]{3,2,1,0:T(8,128)(2,1)} %bitcast.13, s32[]{:T(128)S(6)} %select_n.36, s32[]{:T(128)S(6)} %select_n.34, ...), kind=kLoop, calls=%fused_computation.42 | loop fusion | bytes 2097160 | tf_op jit(solution)/shard_map/jit(dynamic_index_in_dim)/dynamic_slice | solution.py:317
  110.9 8.0 %collective-permute-done.17 = f16[2,2,128,512]{2,3,0,1:T(8,128)(2,1)} collective-permute-done((f16[2,2,128,512]{2,3,0,1:T(8,128)(2,1)}, f16[2,2,128,512]{2,3,0,1:T(8,128)(2,1)}, u32[]{:S(2)}, u32[]{:S(2)}) %collective-permute-start.17) | collective-permute-done | bytes 524320 | tf_op jit(solution)/shard_map/ppermute | solution.py:18
  120.7 8.2 %collective-permute-done.23 = f16[2,2,128,512]{2,3,0,1:T(8,128)(2,1)} collective-permute-done((f16[2,2,128,512]{2,3,0,1:T(8,128)(2,1)}, f16[2,2,128,512]{2,3,0,1:T(8,128)(2,1)}, u32[]{:S(2)}, u32[]{:S(2)}) %collective-permute-start.23) | collective-permute-done | bytes 524320 | tf_op jit(solution)/shard_map/ppermute | solution.py:18
  131.1 7.5 %collective-permute-done.18 = f16[2,128,512]{1,2,0:T(8,128)(2,1)S(1)} collective-permute-done((f16[2,128,512]{1,2,0:T(8,128)(2,1)S(1)}, f16[2,128,512]{1,2,0:T(8,128)(2,1)S(1)}, u32[]{:S(2)}, u32[]{:S(2)}) %collective-permute-start.18) | collective-permute-done | bytes 262176 | tf_op jit(solution)/shard_map/ppermute | solution.py:18
  139.6 3.5 %collective-permute-done.24 = f16[2,128,512]{1,2,0:T(8,128)(2,1)S(1)} collective-permute-done((f16[2,128,512]{1,2,0:T(8,128)(2,1)S(1)}, f16[2,128,512]{1,2,0:T(8,128)(2,1)S(1)}, u32[]{:S(2)}, u32[]{:S(2)}) %collective-permute-start.24) | collective-permute-done | bytes 262176 | tf_op jit(solution)/shard_map/ppermute | solution.py:18
  (119 shorter events, 42.6 us)
Async XLA Ops:
  13.8 25.9 %collective-permute-start.1 = (bf16[512,512]{1,0:T(8,128)(2,1)}, bf16[512,512]{1,0:T(8,128)(2,1)S(1)}, u32[]{:S(2)}, u32[]{:S(2)}) collective-permute-start(bf16[512,512]{1,0:T(8,128)(2,1)} %get-tuple-element.28), channel_id=1, source_target_pairs={{0,2},{2,0},{4,6},{6,4},{8,10},{10,8},{12,14},{14,12},{16,18},{18,... | collective-permute-start | bytes 1572872 | tf_op jit(solution)/shard_map/ppermute | solution.py:18
  16.8 12.9 %collective-permute-start.8 = (f32[8,1152]{1,0:T(8,128)}, f32[8,1152]{1,0:T(8,128)S(1)}, u32[]{:S(2)}, u32[]{:S(2)}) collective-permute-start(f32[8,1152]{1,0:T(8,128)} %get-tuple-element.35), channel_id=1, source_target_pairs={{0,2},{2,0},{4,6},{6,4},{8,10},{10,8},{12,14},{14,12},{16,18},{18,... | collective-permute-start | bytes 110600 | tf_op jit(solution)/shard_map/ppermute | solution.py:18
  16.9 15.4 %collective-permute-start.10 = (f32[8,1152]{1,0:T(8,128)}, f32[8,1152]{1,0:T(8,128)S(1)}, u32[]{:S(2)}, u32[]{:S(2)}) collective-permute-start(f32[8,1152]{1,0:T(8,128)} %get-tuple-element.36), channel_id=1, source_target_pairs={{0,4},{2,6},{4,0},{6,2},{8,12},{10,14},{12,8},{14,10},{16,20},{18,... | collective-permute-start | bytes 110600 | tf_op jit(solution)/shard_map/ppermute | solution.py:18
  30.5 4.0 %collective-permute-start.9 = (f32[8,1152]{1,0:T(8,128)S(1)}, f32[8,1152]{1,0:T(8,128)S(1)}, u32[]{:S(2)}, u32[]{:S(2)}) collective-permute-start(f32[8,1152]{1,0:T(8,128)S(1)} %add.184.group0), channel_id=1, source_target_pairs={{0,4},{2,6},{4,0},{6,2},{8,12},{10,14},{12,8},{14,10},{16,20},{18,... | collective-permute-start | bytes 110600 | tf_op jit(solution)/shard_map/ppermute | solution.py:18
  33.1 4.0 %collective-permute-start.11 = (f32[8,1152]{1,0:T(8,128)S(1)}, f32[8,1152]{1,0:T(8,128)S(1)}, u32[]{:S(2)}, u32[]{:S(2)}) collective-permute-start(f32[8,1152]{1,0:T(8,128)S(1)} %add.186.group1), channel_id=1, source_target_pairs={{0,2},{2,0},{4,6},{6,4},{8,10},{10,8},{12,14},{14,12},{16,18},{18,... | collective-permute-start | bytes 110600 | tf_op jit(solution)/shard_map/ppermute | solution.py:18
  37.0 4.4 %collective-permute-start.12 = (f32[16,1152]{1,0:T(8,128)S(1)}, f32[16,1152]{1,0:T(8,128)S(1)}, u32[]{:S(2)}, u32[]{:S(2)}) collective-permute-start(f32[16,1152]{1,0:T(8,128)S(1)} %pad_maximum_fusion), channel_id=1, source_target_pairs={{0,8},{2,10},{4,12},{6,14},{8,0},{10,2},{12,4},{14,6},{16,24},{18,... | collective-permute-start | bytes 221192 | tf_op jit(solution)/shard_map/ppermute | solution.py:18
  38.7 11.6 %collective-permute-start.4 = (bf16[512,512]{1,0:T(8,128)(2,1)}, bf16[512,512]{1,0:T(8,128)(2,1)S(1)}, u32[]{:S(2)}, u32[]{:S(2)}) collective-permute-start(bf16[512,512]{1,0:T(8,128)(2,1)} %get-tuple-element.30), channel_id=1, source_target_pairs={{0,4},{2,6},{4,0},{6,2},{8,12},{10,14},{12,8},{14,10},{16,20},{18,... | collective-permute-start | bytes 1572872 | tf_op jit(solution)/shard_map/ppermute | solution.py:18
  39.2 12.6 %collective-permute-start = (bf16[512,512]{1,0:T(8,128)(2,1)}, bf16[512,512]{1,0:T(8,128)(2,1)S(1)}, u32[]{:S(2)}, u32[]{:S(2)}) collective-permute-start(bf16[512,512]{1,0:T(8,128)(2,1)} %get-tuple-element.27.refs_0_), channel_id=1, source_target_pairs={{0,1},{1,0},{2,3},{3,2},{4,5},{5,4},{6,7},{7,6},{8,9},{9,8},{10,11... | collective-permute-start | bytes 1572872 | tf_op jit(solution)/shard_map/ppermute | solution.py:18
  39.2 12.9 %collective-permute-start.3 = (bf16[512,512]{1,0:T(8,128)(2,1)}, bf16[512,512]{1,0:T(8,128)(2,1)S(1)}, u32[]{:S(2)}, u32[]{:S(2)}) collective-permute-start(bf16[512,512]{1,0:T(8,128)(2,1)} %get-tuple-element.29.refs_4_), channel_id=1, source_target_pairs={{0,1},{1,0},{2,3},{3,2},{4,5},{5,4},{6,7},{7,6},{8,9},{9,8},{10,11... | collective-permute-start | bytes 1572872 | tf_op jit(solution)/shard_map/ppermute | solution.py:18
  39.7 12.9 %collective-permute-start.2 = (bf16[512,512]{1,0:T(8,128)(2,1)S(1)}, bf16[512,512]{1,0:T(8,128)(2,1)S(1)}, u32[]{:S(2)}, u32[]{:S(2)}) collective-permute-start(bf16[512,512]{1,0:T(8,128)(2,1)S(1)} %collective-permute-done.1.refs_2_), channel_id=1, source_target_pairs={{0,1},{1,0},{2,3},{3,2},{4,5},{5,4},{6,7},{7,6},{8,9},{9,8},{10,11... | collective-permute-start | bytes 1572872 | tf_op jit(solution)/shard_map/ppermute | solution.py:18
  41.5 8.8 %collective-permute-start.13 = (f32[16,1152]{1,0:T(8,128)S(1)}, f32[16,1152]{1,0:T(8,128)S(1)}, u32[]{:S(2)}, u32[]{:S(2)}) collective-permute-start(f32[16,1152]{1,0:T(8,128)S(1)} %fusion.21), channel_id=1, source_target_pairs={{0,16},{2,18},{4,20},{6,22},{8,24},{10,26},{12,28},{14,30},{16,0},... | collective-permute-start | bytes 221192 | tf_op jit(solution)/shard_map/ppermute | solution.py:18
  50.3 6.5 %collective-permute-start.5 = (bf16[512,512]{1,0:T(8,128)(2,1)S(1)}, bf16[512,512]{1,0:T(8,128)(2,1)S(1)}, u32[]{:S(2)}, u32[]{:S(2)}) collective-permute-start(bf16[512,512]{1,0:T(8,128)(2,1)S(1)} %collective-permute-done.4.refs_6_), channel_id=1, source_target_pairs={{0,1},{1,0},{2,3},{3,2},{4,5},{5,4},{6,7},{7,6},{8,9},{9,8},{10,11... | collective-permute-start | bytes 1572872 | tf_op jit(solution)/shard_map/ppermute | solution.py:18
  50.3 15.1 %collective-permute-start.6 = (bf16[512,512]{1,0:T(8,128)(2,1)}, bf16[512,512]{1,0:T(8,128)(2,1)}, u32[]{:S(2)}, u32[]{:S(2)}) collective-permute-start(bf16[512,512]{1,0:T(8,128)(2,1)} %get-tuple-element.33.near0), channel_id=1, source_target_pairs={{0,2},{2,0},{4,6},{6,4},{8,10},{10,8},{12,14},{14,12},{16,18},{18,... | collective-permute-start | bytes 1572872 | tf_op jit(solution)/shard_map/ppermute | solution.py:18
  51.8 15.1 %collective-permute-start.7 = (bf16[512,512]{1,0:T(8,128)(2,1)}, bf16[512,512]{1,0:T(8,128)(2,1)}, u32[]{:S(2)}, u32[]{:S(2)}) collective-permute-start(bf16[512,512]{1,0:T(8,128)(2,1)} %get-tuple-element.34.near1), channel_id=1, source_target_pairs={{0,4},{2,6},{4,0},{6,2},{8,12},{10,14},{12,8},{14,10},{16,20},{18,... | collective-permute-start | bytes 1572872 | tf_op jit(solution)/shard_map/ppermute | solution.py:18
  52.1 31.4 %collective-permute-start.19 = (bf16[512,512]{1,0:T(8,128)(2,1)}, bf16[512,512]{1,0:T(8,128)(2,1)}, u32[]{:S(2)}, u32[]{:S(2)}) collective-permute-start(bf16[512,512]{1,0:T(8,128)(2,1)} %get-tuple-element.43.near0), channel_id=1, source_target_pairs={{0,2},{2,0},{4,6},{6,4},{8,10},{10,8},{12,14},{14,12},{16,18},{18,... | collective-permute-start | bytes 1572872 | tf_op jit(solution)/shard_map/ppermute | solution.py:18
  52.6 30.9 %collective-permute-start.20 = (bf16[512,512]{1,0:T(8,128)(2,1)}, bf16[512,512]{1,0:T(8,128)(2,1)}, u32[]{:S(2)}, u32[]{:S(2)}) collective-permute-start(bf16[512,512]{1,0:T(8,128)(2,1)} %get-tuple-element.44.near1), channel_id=1, source_target_pairs={{0,4},{2,6},{4,0},{6,2},{8,12},{10,14},{12,8},{14,10},{16,20},{18,... | collective-permute-start | bytes 1572872 | tf_op jit(solution)/shard_map/ppermute | solution.py:18
  72.0 24.2 %collective-permute-start.15 = (f16[512,512]{1,0:T(8,128)(2,1)}, f16[512,512]{1,0:T(8,128)(2,1)}, u32[]{:S(2)}, u32[]{:S(2)}) collective-permute-start(f16[512,512]{1,0:T(8,128)(2,1)} %convert_element_type.140), channel_id=1, source_target_pairs={{0,4},{2,6},{4,0},{6,2},{8,12},{10,14},{12,8},{14,10},{16,20},{18,... | collective-permute-start | bytes 1572872 | tf_op jit(solution)/shard_map/ppermute | solution.py:18
  73.2 23.0 %collective-permute-start.16 = (f16[512,512]{1,0:T(8,128)(2,1)}, f16[512,512]{1,0:T(8,128)(2,1)}, u32[]{:S(2)}, u32[]{:S(2)}) collective-permute-start(f16[512,512]{1,0:T(8,128)(2,1)} %convert_element_type.142), channel_id=1, source_target_pairs={{0,2},{2,0},{4,6},{6,4},{8,10},{10,8},{12,14},{14,12},{16,18},{18,... | collective-permute-start | bytes 1572872 | tf_op jit(solution)/shard_map/ppermute | solution.py:18
  90.1 12.3 %collective-permute-start.21 = (f16[512,512]{1,0:T(8,128)(2,1)}, f16[512,512]{1,0:T(8,128)(2,1)}, u32[]{:S(2)}, u32[]{:S(2)}) collective-permute-start(f16[512,512]{1,0:T(8,128)(2,1)} %convert_element_type.152), channel_id=1, source_target_pairs={{0,4},{2,6},{4,0},{6,2},{8,12},{10,14},{12,8},{14,10},{16,20},{18,... | collective-permute-start | bytes 1572872 | tf_op jit(solution)/shard_map/ppermute | solution.py:18
  92.8 12.0 %collective-permute-start.22 = (f16[512,512]{1,0:T(8,128)(2,1)}, f16[512,512]{1,0:T(8,128)(2,1)}, u32[]{:S(2)}, u32[]{:S(2)}) collective-permute-start(f16[512,512]{1,0:T(8,128)(2,1)} %convert_element_type.154), channel_id=1, source_target_pairs={{0,2},{2,0},{4,6},{6,4},{8,10},{10,8},{12,14},{14,12},{16,18},{18,... | collective-permute-start | bytes 1572872 | tf_op jit(solution)/shard_map/ppermute | solution.py:18
  101.0 17.9 %collective-permute-start.17 = (f16[2,2,128,512]{2,3,0,1:T(8,128)(2,1)}, f16[2,2,128,512]{2,3,0,1:T(8,128)(2,1)}, u32[]{:S(2)}, u32[]{:S(2)}) collective-permute-start(f16[2,2,128,512]{2,3,0,1:T(8,128)(2,1)} %fusion), channel_id=1, source_target_pairs={{0,8},{2,10},{4,12},{6,14},{8,0},{10,2},{12,4},{14,6},{16,24},{18,... | collective-permute-start | bytes 1572872 | tf_op jit(solution)/shard_map/ppermute | solution.py:18
  108.5 20.3 %collective-permute-start.23 = (f16[2,2,128,512]{2,3,0,1:T(8,128)(2,1)}, f16[2,2,128,512]{2,3,0,1:T(8,128)(2,1)}, u32[]{:S(2)}, u32[]{:S(2)}) collective-permute-start(f16[2,2,128,512]{2,3,0,1:T(8,128)(2,1)} %fusion.1), channel_id=1, source_target_pairs={{0,8},{2,10},{4,12},{6,14},{8,0},{10,2},{12,4},{14,6},{16,24},{18,... | collective-permute-start | bytes 1572872 | tf_op jit(solution)/shard_map/ppermute | solution.py:18
  120.0 18.6 %collective-permute-start.18 = (f16[2,128,512]{1,2,0:T(8,128)(2,1)S(1)}, f16[2,128,512]{1,2,0:T(8,128)(2,1)S(1)}, u32[]{:S(2)}, u32[]{:S(2)}) collective-permute-start(f16[2,128,512]{1,2,0:T(8,128)(2,1)S(1)} %fusion.19), channel_id=1, source_target_pairs={{0,16},{2,18},{4,20},{6,22},{8,24},{10,26},{12,28},{14,30},{16,0},... | collective-permute-start | bytes 786440 | tf_op jit(solution)/shard_map/ppermute | solution.py:18
  129.9 13.2 %collective-permute-start.24 = (f16[2,128,512]{1,2,0:T(8,128)(2,1)S(1)}, f16[2,128,512]{1,2,0:T(8,128)(2,1)S(1)}, u32[]{:S(2)}, u32[]{:S(2)}) collective-permute-start(f16[2,128,512]{1,2,0:T(8,128)(2,1)S(1)} %fusion.20), channel_id=1, source_target_pairs={{0,16},{2,18},{4,20},{6,22},{8,24},{10,26},{12,28},{14,30},{16,0},... | collective-permute-start | bytes 786440 | tf_op jit(solution)/shard_map/ppermute | solution.py:18
  (22 other events, 154.8 us)
where the time goes:
time: 146 us; the launch traced here: 145 us
  waiting for transfers between devices  58.2 us (40%)
  Pallas kernels  25.1 us (17%)
  starting transfers between devices  24.4 us (17%)
  local copies, waits for them, and re-layouts  23.8 us (16%)
  other arithmetic  13.3 us (9%)
    ppermute x25, waiting for transfers between devices, swap(): return lax.ppermute(value, axis, [(k, k ^ mask) for k in range(size)])  58.2 us
    ppermute x25, starting transfers between devices, swap(): return lax.ppermute(value, axis, [(k, k ^ mask) for k in range(size)])  24.4 us
    unnamed x58, local copies, waits for them, and re-layouts  17.6 us
    pallas_call x1, Pallas kernels, select_all(): pl.pallas_call(select_kernel, out_shape=[jax.ShapeDtypeStruct((images, wi...  13.8 us
    pallas_call x2, Pallas kernels, product(): pl.pallas_call(product_kernel, grid=(1,), out_shape=[out] * (2 * PAIRS),...  8.34 us
    dynamic_slice x4, local copies, waits for them, and re-layouts, pick(): return lax.dynamic_index_in_dim(value, at, axis, keepdims=False)  6.16 us
    convert_element_type x4, other arithmetic, fast(): values[p].astype(jnp.float16)  3.61 us
  transfers between devices with their start and end apart: 25, of which 12 were waited for; matrix products, arithmetic and copies ran while one was open for 21% of the time, Pallas kernels for 8%

commit v1 on v0

--- a/solution.py
+++ b/solution.py
@@ -8,7 +8,8 @@
 VIEWS = 10
 PAIRS = 2
 EPS = 1e-05
-CHUNKS = 2
+CHUNKS = 4
+PARTS = 2
 STEPS = 10
 UNIT = 16384.0
 
@@ -102,7 +103,7 @@
 
     lax.fori_loop(0, groups, gather, 0)
     me = lax.axis_index("dp")
-    mine = [jnp.bitwise_and(jnp.right_shift(me, bit), 1) for bit in range(2)]
+    mine = [jnp.bitwise_and(jnp.right_shift(me, bit), 1) for bit in range(4)]
     span = width // CHUNKS // 128
     for k in range(4):
         p, line = k // 2, 2 * (k % 2)
@@ -111,7 +112,8 @@
                 near, over, rest = m // 4, (m // 2) % 2, m % 2
                 near_value = mine[p] if near else 1 - mine[p]
                 over_value = mine[1 - p] if over else 1 - mine[1 - p]
-                c = rest * 4 + near_value * (1 << p) + over_value * (2 >> p)
+                rest_value = mine[2] if rest else 1 - mine[2]
+                c = rest_value * 4 + near_value * (1 << p) + over_value * (2 >> p)
                 out = (kept if near else away)[p]
                 lane = (m % 4) * 128
             else:
@@ -157,18 +159,24 @@
     )(slot_image.reshape(1, -1), slot_view.reshape(1, -1), pair_table, embeddings)
 
 
+def kept_core():
+    return jnp.bitwise_and(jnp.right_shift(lax.axis_index("dp"), 3), 1) == lax.axis_index("feat")
+
+
 def turn_kernel(*refs):
+    own_at = jnp.where(kept_core(), 1, 0)
     for p in range(PAIRS):
         kept, kept_other, come, come_other = refs[4 * p : 4 * p + 4]
         out = refs[4 * PAIRS + p]
-        images, half = kept.shape[0], kept.shape[1] // 2
+        images, block = kept.shape[0], kept.shape[1] // 4
         for column, sources in enumerate(((kept, kept_other), (come, come_other))):
-            for line in range(2):
+            for m in range(4):
                 for s in range(2):
-                    row = (2 * line + s) * half
-                    out[row : row + half, column * images : (column + 1) * images] = jnp.transpose(
-                        sources[s][:, line * half : (line + 1) * half]
-                    )
+                    at = (2 * m + (1 - own_at if s else own_at)) * block
+                    out[
+                        pl.ds(pl.multiple_of(at, block), block),
+                        column * images : (column + 1) * images,
+                    ] = jnp.transpose(sources[s][:, m * block : (m + 1) * block])
 
 
 def turn(operands):
@@ -188,7 +196,7 @@
 def moment_kernel(total_ref, group0, group1, rows_ref, lines_ref, work):
     width = rows_ref.shape[1]
     me = lax.axis_index("dp")
-    mine = [jnp.bitwise_and(jnp.right_shift(me, bit), 1) for bit in range(2)]
+    mine = [jnp.bitwise_and(jnp.right_shift(me, bit), 1) for bit in range(4)]
     rows_ref[...] = jnp.zeros_like(rows_ref)
     lines_ref[...] = jnp.zeros_like(lines_ref)
     for p, group in enumerate((group0, group1)):
@@ -209,7 +217,8 @@
         work[2:3, :] = 1.0 / roots[1]
         for m in range(4):
             over_value = mine[1 - p] if m // 2 else 1 - mine[1 - p]
-            c = (m % 2) * 4 + mine[p] * (1 << p) + over_value * (2 >> p)
+            rest_value = mine[2] if m % 2 else 1 - mine[2]
+            c = rest_value * 4 + mine[p] * (1 << p) + over_value * (2 >> p)
             lines_ref[8 * p : 8 * p + 3, m * 128 : (m + 1) * 128] = work[
                 0:3, pl.ds(pl.multiple_of(c * 128, 128), 128)
             ]
@@ -233,24 +242,28 @@
 
 def product_kernel(turned0, turned1, near0, far0, near1, far1, rows_ref, lines, lines_other, *outs):
     go, stay = outs[:PAIRS], outs[PAIRS:]
+    own_kept = kept_core()
     for p, (turned, near, far) in enumerate(((turned0, near0, far0), (turned1, near1, far1))):
-        depth = near.shape[0]
-        half = lines.shape[1] // 2
+        block = lines.shape[1] // 4
         own, other = lines[8 * p : 8 * p + 8, :], lines_other[8 * p : 8 * p + 8, :]
+        sources = (jnp.where(own_kept, other, own), jnp.where(own_kept, own, other))
         mean = rows_ref[8 * p : 8 * p + 1, :]
         shift = rows_ref[8 * p + 1 : 8 * p + 2, :]
         rate = rows_ref[8 * p + 2 : 8 * p + 3, :]
-        for part in range(4):
-            side, s = part // 2, part % 2
-            rows = slice(part * half, (part + 1) * half)
-            value = jnp.dot(turned[rows, :depth], near[...], preferred_element_type=jnp.float32)
-            value += jnp.dot(turned[rows, depth:], far[...], preferred_element_type=jnp.float32)
-            column = jnp.transpose((other if s else own)[:, side * half : (side + 1) * half])
+        right = jnp.concatenate([near[...], far[...]], 0)
+        for part in range(8):
+            m, z = part // 2, part % 2
+            value = jnp.dot(
+                turned[part * block : (part + 1) * block, :], right, preferred_element_type=jnp.float32
+            )
+            column = jnp.transpose(sources[z][:, m * block : (m + 1) * block])
             value = value - column[:, 0:1] * mean - column[:, 1:2] * shift
             value = value * (column[:, 2:3] * rate)
-            if side == 0:
+            if part < 4:
                 value = jnp.clip(value, -60000.0, 60000.0)
-            (stay if side else go)[p][s * half : (s + 1) * half, :] = value
+                go[p][part * block : (part + 1) * block, :] = value
+            else:
+                stay[p][(part - 4) * block : (part - 3) * block, :] = value
 
 
 def product(turned, near, far, rows, lines, lines_other, c):
@@ -272,10 +285,28 @@
     )(*turned, near[0], far[0], near[1], far[1], rows, lines, lines_other)
 
 
+def finish_kernel(*refs):
+    out = refs[-1]
+    chunk = refs[0].shape[2]
+    for c, ref in enumerate(refs[:-1]):
+        for p in range(PAIRS):
+            out[p, c * chunk : (c + 1) * chunk, :] = jnp.transpose(ref[p]) * (1.0 / UNIT)
+
+
+def finish(parts):
+    pairs, block, chunk = parts[0].shape
+    vmem = pl.BlockSpec(memory_space=pltpu.VMEM)
+    return pl.pallas_call(
+        finish_kernel,
+        out_shape=jax.ShapeDtypeStruct((pairs, chunk * len(parts), block), jnp.float32),
+        in_specs=[vmem] * len(parts),
+        out_specs=vmem,
+        name="finish",
+    )(*parts)
+
+
 def fast(embeddings, slot_image, slot_view, pair_table, images):
     width = embeddings.shape[1]
-    me, core = lax.axis_index("dp"), lax.axis_index("feat")
-    mine = [(me >> bit) & 1 for bit in range(4)]
     block = 128
     chosen = select_all(embeddings, slot_image, slot_view, pair_table, images)
     firsts = (chosen[:CHUNKS], chosen[CHUNKS : 2 * CHUNKS])
@@ -305,28 +336,24 @@
             lines_other,
             c,
         )
-        chunk = width // CHUNKS
-        shape = (2, 2, block, chunk)
-        sent = [
-            swap(values[p].astype(jnp.float16), "dp", over_bit[p]).reshape(shape)
-            for p in range(PAIRS)
-        ]
-        stay = [values[PAIRS + p].reshape(shape) for p in range(PAIRS)]
-
-        def pick(value, at, axis):
-            return lax.dynamic_index_in_dim(value, at, axis, keepdims=False)
-
-        def merge(own, other, at, axis):
-            return pick(own, at, axis) + pick(other, at, axis).astype(jnp.float32)
-
-        go = jnp.stack([merge(stay[p], sent[p], 1 - mine[2], 1) for p in range(PAIRS)])
-        go = swap(jnp.clip(go, -60000.0, 60000.0).astype(jnp.float16), "dp", 4)
-        stay = jnp.stack([merge(stay[p], sent[p], mine[2], 1) for p in range(PAIRS)])
-        keep_at = mine[3] ^ core
-        last = jnp.clip(merge(stay, go, 1 - keep_at, 1), -60000.0, 60000.0).astype(jnp.float16)
+        sent = [swap(values[p].astype(jnp.float16), "dp", over_bit[p]) for p in range(PAIRS)]
+        both = range(PAIRS)
+
+        def narrow(value):
+            return jnp.clip(value, -60000.0, 60000.0).astype(jnp.float16)
+
+        def merge(p, at):
+            return values[PAIRS + p][at] + sent[p][at].astype(jnp.float32)
+
+        head, rest = slice(0, 2 * block), slice(2 * block, 4 * block)
+        go = swap(jnp.stack([narrow(merge(p, head)) for p in both]), "dp", 4)
+        stay = jnp.stack([merge(p, rest) for p in both])
+        last = narrow(stay[:, :block] + go[:, :block].astype(jnp.float32))
         last = swap(last, "dp", 8)
-        finals.append(merge(stay, go, keep_at, 1) + last.astype(jnp.float32))
-    return jnp.swapaxes(jnp.concatenate(finals, 2), 1, 2) * (1.0 / UNIT)
+        finals.append(
+            stay[:, block:] + go[:, block:].astype(jnp.float32) + last.astype(jnp.float32)
+        )
+    return finish(finals)
 
 
 def select_plain(embeddings, slot_image, slot_view, pair_table, images):
@@ -366,7 +393,7 @@
     block = width * feat // dp
     low, high = bits_of(width // block), bits_of(feat)
     mine = [(me >> bit) & 1 for bit in range(low + high)]
-    chunk = width // CHUNKS
+    chunk = width // PARTS
     orders = []
     for p in range(PAIRS):
         order = list(range(low + high))
@@ -402,9 +429,9 @@
     totals = list(group)
     for step in range(1, low + high):
         totals = [totals[p] + swap(totals[p], "dp", 1 << orders[p][step]) for p in range(PAIRS)]
-    pieces = [[firsts[p][:, c * chunk : (c + 1) * chunk] for c in range(CHUNKS)] for p in range(PAIRS)]
-    far = [[None] * CHUNKS for _ in range(PAIRS)]
-    for c in range(CHUNKS):
+    pieces = [[firsts[p][:, c * chunk : (c + 1) * chunk] for c in range(PARTS)] for p in range(PAIRS)]
+    far = [[None] * PARTS for _ in range(PAIRS)]
+    for c in range(PARTS):
         for p in range(PAIRS):
             far[p][c] = swap(pieces[p][c], "dp", 1 << orders[p][0])
     kept_all = [across(kept[p]) for p in range(PAIRS)]
@@ -442,8 +469,8 @@
     def narrow(value):
         return jnp.clip(value, -60000.0, 60000.0).astype(jnp.float16)
 
-    stay = [[None] * CHUNKS for _ in range(PAIRS)]
-    for c in range(CHUNKS):
+    stay = [[None] * PARTS for _ in range(PAIRS)]
+    for c in range(PARTS):
         for p in range(PAIRS):
             sent = swap(narrow(product(p, c, 0)), "dp", 1 << orders[p][1])
             stay[p][c] = product(p, c, 1) + sent.astype(jnp.float32)
@@ -452,14 +479,14 @@
         axis = axes.index(bit)
         axes.remove(bit)
         keep_at = mine[bit] ^ ((core >> (bit - low)) & 1) if bit >= low else mine[bit]
-        for c in range(CHUNKS):
+        for c in range(PARTS):
             for p in range(PAIRS):
                 go = lax.dynamic_index_in_dim(stay[p][c], 1 - keep_at, axis, keepdims=False)
                 sent = swap(narrow(go), "dp", 1 << bit)
                 own = lax.dynamic_index_in_dim(stay[p][c], keep_at, axis, keepdims=False)
                 stay[p][c] = own + sent.astype(jnp.float32)
     return jnp.stack(
-        [jnp.concatenate([stay[p][c].T for c in range(CHUNKS)], 0) for p in range(PAIRS)]
+        [jnp.concatenate([stay[p][c].T for c in range(PARTS)], 0) for p in range(PAIRS)]
     ) * (1.0 / UNIT)
 
 
@@ -469,4 +496,5 @@
     step = jax.shard_map(local, mesh=mesh, in_specs=in_specs, out_specs=out_specs, check_vma=False)
     if dict(mesh.shape) != {"dp": 16, "feat": 2}:
         return step
+
     return step

time: 146 us -> 136 us (0.932)
  local copies, waits for them, and re-layouts: 23.8 us -> 2.13 us
  starting transfers between devices: 24.4 us -> 43.3 us
  other arithmetic: 13.3 us -> 6.45 us
    ppermute x25 -> x37, starting transfers between devices: 24.4 us -> 43.3 us  [swap(): return lax.ppermute(value, axis, [(k, k ^ mask) for k in range(size)])]
    unnamed x58 -> x28, local copies, waits for them, and re-layouts: 17.6 us -> 2.13 us
    dynamic_slice x4 -> x0, local copies, waits for them, and re-layouts: 6.16 us -> none  [pick(): return lax.dynamic_index_in_dim(value, at, axis, keepdims=False)]
    convert_element_type x4, other arithmetic: 3.88 us -> 0.17 us  [narrow(): return jnp.clip(value, -60000.0, 60000.0).astype(jnp.float16)]
    convert_element_type x4 -> x8, other arithmetic: 3.61 us -> 0.32 us  [fast(): values[p].astype(jnp.float16)]
    pallas_call x0 -> x1, Pallas kernels: none -> 2.49 us  [finish(): pl.pallas_call(finish_kernel, out_shape=jax.ShapeDtypeStruct((pairs, chun...]
    pallas_call x2 -> x4, Pallas kernels: 8.34 us -> 6.28 us  [product(): pl.pallas_call(product_kernel, grid=(1,), out_shape=[out] * (2 * PAIRS),...]
    add x10 -> x4, other arithmetic: 2.5 us -> 2.99 us  [fast(): stay[:, block:] + go[:, block:].astype(jnp.float32)]
  transfers between devices with their start and end apart: 25 -> 37, of which waited for: 12 -> 21; matrix products, arithmetic and copies ran while one was open for 21% -> 4% of each run, Pallas kernels for 8% -> 7%
where the time goes in v1:
time: 136 us
  waiting for transfers between devices  58.3 us (43%)
  starting transfers between devices  43.3 us (32%)
  Pallas kernels  25.4 us (19%)
  other arithmetic  6.45 us (5%)
  local copies, waits for them, and re-layouts  2.13 us (2%)
    ppermute x37, waiting for transfers between devices, swap(): return lax.ppermute(value, axis, [(k, k ^ mask) for k in range(size)])  58.3 us
    ppermute x37, starting transfers between devices, swap(): return lax.ppermute(value, axis, [(k, k ^ mask) for k in range(size)])  43.3 us
    pallas_call x1, Pallas kernels, select_all(): pl.pallas_call(select_kernel, out_shape=[jax.ShapeDtypeStruct((images, wi...  13.7 us
    pallas_call x4, Pallas kernels, product(): pl.pallas_call(product_kernel, grid=(1,), out_shape=[out] * (2 * PAIRS),...  6.28 us
    add x4, other arithmetic, fast(): stay[:, block:] + go[:, block:].astype(jnp.float32)  2.99 us
  transfers between devices with their start and end apart: 37, of which 21 were waited for; matrix products, arithmetic and copies ran while one was open for 4% of the time, Pallas kernels for 7%

profile of v1, /device:TPU:0, one launch (start us, length us, event | category | flops | bytes accessed | tf_op | source)
XLA Modules:
  0.0 135.9 jit_solution(10241945994834014715)
XLA Ops:
  0.0 13.7 %select.1 = (bf16[512,256]{1,0:T(8,128)(2,1)}, bf16[512,256]{1,0:T(8,128)(2,1)}, bf16[512,256]{1,0:T(8,128)(2,1)}, bf16[512,256]{1,0:T(8,128)(2,1)}, bf16[512,25...) custom-call(s32[1,5120]{1,0:T(1,128)} %bitcast.34, ...), custom_call_target="tpu_custom_call" | custom-call | tf_op jit(solution)/shard_map/select/pallas_call | solution.py:141
  13.7 3.1 %collective-permute-start.10 = (f32[8,1152]{1,0:T(8,128)}, f32[8,1152]{1,0:T(8,128)S(1)}, u32[]{:S(2)}, u32[]{:S(2)}) collective-permute-start(f32[8,1152]{1,0:T(8,128)} %get-tuple-element.48), channel_id=1, source_target_pairs={{0,4},{2,6},{4,0},{6,2},{8,12},{10,14},{12,8},{14,10},{16,20},{18,... | collective-permute-start | bytes 110600 | tf_op jit(solution)/shard_map/ppermute | solution.py:19
  19.7 2.0 %collective-permute-start.11 = (f32[8,1152]{1,0:T(8,128)S(1)}, f32[8,1152]{1,0:T(8,128)S(1)}, u32[]{:S(2)}, u32[]{:S(2)}) collective-permute-start(f32[8,1152]{1,0:T(8,128)S(1)} %add.104.group1), channel_id=1, source_target_pairs={{0,2},{2,0},{4,6},{6,4},{8,10},{10,8},{12,14},{14,12},{16,18},{18,... | collective-permute-start | bytes 110600 | tf_op jit(solution)/shard_map/ppermute | solution.py:19
  24.0 2.4 %collective-permute-done.9 = f32[8,1152]{1,0:T(8,128)S(1)} collective-permute-done((f32[8,1152]{1,0:T(8,128)S(1)}, f32[8,1152]{1,0:T(8,128)S(1)}, u32[]{:S(2)}, u32[]{:S(2)}) %collective-permute-start.9) | collective-permute-done | bytes 36896 | tf_op jit(solution)/shard_map/ppermute | solution.py:19
  26.5 1.6 %collective-permute-start.12 = (f32[16,1152]{1,0:T(8,128)S(1)}, f32[16,1152]{1,0:T(8,128)S(1)}, u32[]{:S(2)}, u32[]{:S(2)}) collective-permute-start(f32[16,1152]{1,0:T(8,128)S(1)} %pad_maximum_fusion.8), channel_id=1, source_target_pairs={{0,8},{2,10},{4,12},{6,14},{8,0},{10,2},{12,4},{14,6},{16,24},{18,... | collective-permute-start | bytes 221192 | tf_op jit(solution)/shard_map/ppermute | solution.py:19
  30.9 2.7 %collective-permute-start.13 = (f32[16,1152]{1,0:T(8,128)S(1)}, f32[16,1152]{1,0:T(8,128)S(1)}, u32[]{:S(2)}, u32[]{:S(2)}) collective-permute-start(f32[16,1152]{1,0:T(8,128)S(1)} %fusion.32), channel_id=1, source_target_pairs={{0,16},{2,18},{4,20},{6,22},{8,24},{10,26},{12,28},{14,30},{16,0},... | collective-permute-start | bytes 221192 | tf_op jit(solution)/shard_map/ppermute | solution.py:19
  33.6 5.9 %collective-permute-done.1.refs_2_ = bf16[512,512]{1,0:T(8,128)(2,1)S(1)} collective-permute-done((bf16[512,512]{1,0:T(8,128)(2,1)}, bf16[512,512]{1,0:T(8,128)(2,1)S(1)}, u32[]{:S(2)}, u32[]{:S(2)}) %collective-permute-start.1) | collective-permute-done | bytes 524320 | tf_op jit(solution)/shard_map/ppermute | solution.py:19
  40.6 1.7 %moments.1 = (f32[16,1024]{1,0:T(8,128)}, f32[16,512]{1,0:T(8,128)}) custom-call(f32[16,1152]{1,0:T(8,128)} %add.107.total_ref, f32[8,1152]{1,0:T(8,128)} %copy-done.13, f32[8,1152]{1,0:T(8,128)} %copy-done.12), custom_call_target="tpu_custom_call" | custom-call | bytes 409600 | tf_op jit(solution)/shard_map/moments/pallas_call | solution.py:229
  45.1 7.4 %collective-permute-done.6.far0 = bf16[512,256]{1,0:T(8,128)(2,1)S(1)} collective-permute-done((bf16[512,256]{1,0:T(8,128)(2,1)}, bf16[512,256]{1,0:T(8,128)(2,1)S(1)}, u32[]{:S(2)}, u32[]{:S(2)}) %collective-permute-start.6) | collective-permute-done | bytes 262176 | tf_op jit(solution)/shard_map/ppermute | solution.py:19
  70.5 1.6 %collective-permute-start.16 = (f16[512,256]{1,0:T(8,128)(2,1)S(1)}, f16[512,256]{1,0:T(8,128)(2,1)S(1)}, u32[]{:S(2)}, u32[]{:S(2)}) collective-permute-start(f16[512,256]{1,0:T(8,128)(2,1)S(1)} %convert_element_type.146), channel_id=1, source_target_pairs={{0,2},{2,0},{4,6},{6,4},{8,10},{10,8},{12,14},{14,12},{16,18},{18,... | collective-permute-start | bytes 786440 | tf_op jit(solution)/shard_map/ppermute | solution.py:19
  76.1 1.6 %collective-permute-start.22 = (f16[512,256]{1,0:T(8,128)(2,1)S(1)}, f16[512,256]{1,0:T(8,128)(2,1)S(1)}, u32[]{:S(2)}, u32[]{:S(2)}) collective-permute-start(f16[512,256]{1,0:T(8,128)(2,1)S(1)} %convert_element_type.158), channel_id=1, source_target_pairs={{0,2},{2,0},{4,6},{6,4},{8,10},{10,8},{12,14},{14,12},{16,18},{18,... | collective-permute-start | bytes 786440 | tf_op jit(solution)/shard_map/ppermute | solution.py:19
  81.8 2.6 %collective-permute-done.15 = f16[512,256]{1,0:T(8,128)(2,1)S(1)} collective-permute-done((f16[512,256]{1,0:T(8,128)(2,1)S(1)}, f16[512,256]{1,0:T(8,128)(2,1)S(1)}, u32[]{:S(2)}, u32[]{:S(2)}) %collective-permute-start.15) | collective-permute-done | bytes 262176 | tf_op jit(solution)/shard_map/ppermute | solution.py:19
  85.8 1.6 %collective-permute-start.33 = (f16[512,256]{1,0:T(8,128)(2,1)S(1)}, f16[512,256]{1,0:T(8,128)(2,1)S(1)}, u32[]{:S(2)}, u32[]{:S(2)}) collective-permute-start(f16[512,256]{1,0:T(8,128)(2,1)S(1)} %convert_element_type.180), channel_id=1, source_target_pairs={{0,4},{2,6},{4,0},{6,2},{8,12},{10,14},{12,8},{14,10},{16,20},{18,... | collective-permute-start | bytes 786440 | tf_op jit(solution)/shard_map/ppermute | solution.py:19
  87.6 2.4 %collective-permute-done.21 = f16[512,256]{1,0:T(8,128)(2,1)S(1)} collective-permute-done((f16[512,256]{1,0:T(8,128)(2,1)S(1)}, f16[512,256]{1,0:T(8,128)(2,1)S(1)}, u32[]{:S(2)}, u32[]{:S(2)}) %collective-permute-start.21) | collective-permute-done | bytes 262176 | tf_op jit(solution)/shard_map/ppermute | solution.py:19
  92.0 3.6 %collective-permute-done.27 = f16[512,256]{1,0:T(8,128)(2,1)S(1)} collective-permute-done((f16[512,256]{1,0:T(8,128)(2,1)S(1)}, f16[512,256]{1,0:T(8,128)(2,1)S(1)}, u32[]{:S(2)}, u32[]{:S(2)}) %collective-permute-start.27) | collective-permute-done | bytes 262176 | tf_op jit(solution)/shard_map/ppermute | solution.py:19
  96.3 1.6 %collective-permute-start.29 = (f16[2,256,256]{2,1,0:T(8,128)(2,1)S(1)}, f16[2,256,256]{2,1,0:T(8,128)(2,1)S(1)}, u32[]{:S(2)}, u32[]{:S(2)}) collective-permute-start(f16[2,256,256]{2,1,0:T(8,128)(2,1)S(1)} %pad_maximum_fusion.6), channel_id=1, source_target_pairs={{0,8},{2,10},{4,12},{6,14},{8,0},{10,2},{12,4},{14,6},{16,24},{18,... | collective-permute-start | bytes 786440 | tf_op jit(solution)/shard_map/ppermute | solution.py:19
  97.9 1.8 %collective-permute-done.33 = f16[512,256]{1,0:T(8,128)(2,1)S(1)} collective-permute-done((f16[512,256]{1,0:T(8,128)(2,1)S(1)}, f16[512,256]{1,0:T(8,128)(2,1)S(1)}, u32[]{:S(2)}, u32[]{:S(2)}) %collective-permute-start.33) | collective-permute-done | bytes 262176 | tf_op jit(solution)/shard_map/ppermute | solution.py:19
  100.5 2.7 %collective-permute-start.18 = (f16[2,128,256]{2,1,0:T(8,128)(2,1)S(1)}, f16[2,128,256]{2,1,0:T(8,128)(2,1)S(1)}, u32[]{:S(2)}, u32[]{:S(2)}) collective-permute-start(f16[2,128,256]{2,1,0:T(8,128)(2,1)S(1)} %fusion.23), channel_id=1, source_target_pairs={{0,16},{2,18},{4,20},{6,22},{8,24},{10,26},{12,28},{14,30},{16,0},... | collective-permute-start | bytes 393224 | tf_op jit(solution)/shard_map/ppermute | solution.py:19
  103.2 7.1 %collective-permute-done.23 = f16[2,256,256]{2,1,0:T(8,128)(2,1)S(1)} collective-permute-done((f16[2,256,256]{2,1,0:T(8,128)(2,1)S(1)}, f16[2,256,256]{2,1,0:T(8,128)(2,1)S(1)}, u32[]{:S(2)}, u32[]{:S(2)}) %collective-permute-start.23) | collective-permute-done | bytes 262176 | tf_op jit(solution)/shard_map/ppermute | solution.py:19
  110.9 6.3 %collective-permute-done.29 = f16[2,256,256]{2,1,0:T(8,128)(2,1)S(1)} collective-permute-done((f16[2,256,256]{2,1,0:T(8,128)(2,1)S(1)}, f16[2,256,256]{2,1,0:T(8,128)(2,1)S(1)}, u32[]{:S(2)}, u32[]{:S(2)}) %collective-permute-start.29) | collective-permute-done | bytes 262176 | tf_op jit(solution)/shard_map/ppermute | solution.py:19
  117.4 4.1 %collective-permute-done.35 = f16[2,256,256]{2,1,0:T(8,128)(2,1)S(1)} collective-permute-done((f16[2,256,256]{2,1,0:T(8,128)(2,1)S(1)}, f16[2,256,256]{2,1,0:T(8,128)(2,1)S(1)}, u32[]{:S(2)}, u32[]{:S(2)}) %collective-permute-start.35) | collective-permute-done | bytes 262176 | tf_op jit(solution)/shard_map/ppermute | solution.py:19
  122.3 6.2 %collective-permute-done.24 = f16[2,128,256]{2,1,0:T(8,128)(2,1)S(1)} collective-permute-done((f16[2,128,256]{2,1,0:T(8,128)(2,1)S(1)}, f16[2,128,256]{2,1,0:T(8,128)(2,1)S(1)}, u32[]{:S(2)}, u32[]{:S(2)}) %collective-permute-start.24) | collective-permute-done | bytes 131104 | tf_op jit(solution)/shard_map/ppermute | solution.py:19
  129.3 1.9 %collective-permute-done.30 = f16[2,128,256]{2,1,0:T(8,128)(2,1)S(1)} collective-permute-done((f16[2,128,256]{2,1,0:T(8,128)(2,1)S(1)}, f16[2,128,256]{2,1,0:T(8,128)(2,1)S(1)}, u32[]{:S(2)}, u32[]{:S(2)}) %collective-permute-start.30) | collective-permute-done | bytes 131104 | tf_op jit(solution)/shard_map/ppermute | solution.py:19
  133.4 2.5 %finish.1 = f32[2,1024,128]{2,1,0:T(8,128)} custom-call(f32[2,128,256]{2,1,0:T(8,128)} %fusion.11.refs_0_, f32[2,128,256]{2,1,0:T(8,128)} %fusion.8.refs_1_, f32[2,128,256]{2,1,0:T(8,128)} %fusion.5.refs_2_, f32[2,128,256]{2,1,0:T(8,128)} %fusion.2.refs_3_), custom_call_target="tpu_custom_call" | custom-call | tf_op jit(solution)/shard_map/finish/pallas_call | solution.py:299
  (121 shorter events, 47.4 us)
Async XLA Ops:
  28.1 11.3 %collective-permute-start.1 = (bf16[512,512]{1,0:T(8,128)(2,1)}, bf16[512,512]{1,0:T(8,128)(2,1)S(1)}, u32[]{:S(2)}, u32[]{:S(2)}) collective-permute-start(bf16[512,512]{1,0:T(8,128)(2,1)} %get-tuple-element.40), channel_id=1, source_target_pairs={{0,2},{2,0},{4,6},{6,4},{8,10},{10,8},{12,14},{14,12},{16,18},{18,... | collective-permute-start | bytes 1572872 | tf_op jit(solution)/shard_map/ppermute | solution.py:19
  30.2 23.7 %collective-permute-start = (bf16[512,512]{1,0:T(8,128)(2,1)}, bf16[512,512]{1,0:T(8,128)(2,1)S(1)}, u32[]{:S(2)}, u32[]{:S(2)}) collective-permute-start(bf16[512,512]{1,0:T(8,128)(2,1)} %get-tuple-element.39.refs_0_), channel_id=1, source_target_pairs={{0,1},{1,0},{2,3},{3,2},{4,5},{5,4},{6,7},{7,6},{8,9},{9,8},{10,11... | collective-permute-start | bytes 1572872 | tf_op jit(solution)/shard_map/ppermute | solution.py:19
  30.2 25.3 %collective-permute-start.3 = (bf16[512,512]{1,0:T(8,128)(2,1)}, bf16[512,512]{1,0:T(8,128)(2,1)S(1)}, u32[]{:S(2)}, u32[]{:S(2)}) collective-permute-start(bf16[512,512]{1,0:T(8,128)(2,1)} %get-tuple-element.41.refs_4_), channel_id=1, source_target_pairs={{0,1},{1,0},{2,3},{3,2},{4,5},{5,4},{6,7},{7,6},{8,9},{9,8},{10,11... | collective-permute-start | bytes 1572872 | tf_op jit(solution)/shard_map/ppermute | solution.py:19
  39.4 16.5 %collective-permute-start.2 = (bf16[512,512]{1,0:T(8,128)(2,1)S(1)}, bf16[512,512]{1,0:T(8,128)(2,1)S(1)}, u32[]{:S(2)}, u32[]{:S(2)}) collective-permute-start(bf16[512,512]{1,0:T(8,128)(2,1)S(1)} %collective-permute-done.1.refs_2_), channel_id=1, source_target_pairs={{0,1},{1,0},{2,3},{3,2},{4,5},{5,4},{6,7},{7,6},{8,9},{9,8},{10,11... | collective-permute-start | bytes 1572872 | tf_op jit(solution)/shard_map/ppermute | solution.py:19
  39.8 16.8 %collective-permute-start.5 = (bf16[512,512]{1,0:T(8,128)(2,1)S(1)}, bf16[512,512]{1,0:T(8,128)(2,1)S(1)}, u32[]{:S(2)}, u32[]{:S(2)}) collective-permute-start(bf16[512,512]{1,0:T(8,128)(2,1)S(1)} %collective-permute-done.4.refs_6_), channel_id=1, source_target_pairs={{0,1},{1,0},{2,3},{3,2},{4,5},{5,4},{6,7},{7,6},{8,9},{9,8},{10,11... | collective-permute-start | bytes 1572872 | tf_op jit(solution)/shard_map/ppermute | solution.py:19
  55.4 12.1 %collective-permute-start.20 = (bf16[512,256]{1,0:T(8,128)(2,1)}, bf16[512,256]{1,0:T(8,128)(2,1)S(1)}, u32[]{:S(2)}, u32[]{:S(2)}) collective-permute-start(bf16[512,256]{1,0:T(8,128)(2,1)} %get-tuple-element.56.near1), channel_id=1, source_target_pairs={{0,4},{2,6},{4,0},{6,2},{8,12},{10,14},{12,8},{14,10},{16,20},{18,... | collective-permute-start | bytes 786440 | tf_op jit(solution)/shard_map/ppermute | solution.py:19
  55.9 14.6 %collective-permute-start.25 = (bf16[512,256]{1,0:T(8,128)(2,1)}, bf16[512,256]{1,0:T(8,128)(2,1)S(1)}, u32[]{:S(2)}, u32[]{:S(2)}) collective-permute-start(bf16[512,256]{1,0:T(8,128)(2,1)} %get-tuple-element.61.near0), channel_id=1, source_target_pairs={{0,2},{2,0},{4,6},{6,4},{8,10},{10,8},{12,14},{14,12},{16,18},{18,... | collective-permute-start | bytes 786440 | tf_op jit(solution)/shard_map/ppermute | solution.py:19
  56.6 16.6 %collective-permute-start.26 = (bf16[512,256]{1,0:T(8,128)(2,1)}, bf16[512,256]{1,0:T(8,128)(2,1)S(1)}, u32[]{:S(2)}, u32[]{:S(2)}) collective-permute-start(bf16[512,256]{1,0:T(8,128)(2,1)} %get-tuple-element.62.near1), channel_id=1, source_target_pairs={{0,4},{2,6},{4,0},{6,2},{8,12},{10,14},{12,8},{14,10},{16,20},{18,... | collective-permute-start | bytes 786440 | tf_op jit(solution)/shard_map/ppermute | solution.py:19
  61.9 14.2 %collective-permute-start.31 = (bf16[512,256]{1,0:T(8,128)(2,1)S(1)}, bf16[512,256]{1,0:T(8,128)(2,1)S(1)}, u32[]{:S(2)}, u32[]{:S(2)}) collective-permute-start(bf16[512,256]{1,0:T(8,128)(2,1)S(1)} %copy-done.4), channel_id=1, source_target_pairs={{0,2},{2,0},{4,6},{6,4},{8,10},{10,8},{12,14},{14,12},{16,18},{18,... | collective-permute-start | bytes 786440 | tf_op jit(solution)/shard_map/ppermute | solution.py:19
  63.3 15.4 %collective-permute-start.32 = (bf16[512,256]{1,0:T(8,128)(2,1)S(1)}, bf16[512,256]{1,0:T(8,128)(2,1)S(1)}, u32[]{:S(2)}, u32[]{:S(2)}) collective-permute-start(bf16[512,256]{1,0:T(8,128)(2,1)S(1)} %copy-done.5), channel_id=1, source_target_pairs={{0,4},{2,6},{4,0},{6,2},{8,12},{10,14},{12,8},{14,10},{16,20},{18,... | collective-permute-start | bytes 786440 | tf_op jit(solution)/shard_map/ppermute | solution.py:19
  67.5 16.9 %collective-permute-start.15 = (f16[512,256]{1,0:T(8,128)(2,1)S(1)}, f16[512,256]{1,0:T(8,128)(2,1)S(1)}, u32[]{:S(2)}, u32[]{:S(2)}) collective-permute-start(f16[512,256]{1,0:T(8,128)(2,1)S(1)} %convert_element_type.144), channel_id=1, source_target_pairs={{0,4},{2,6},{4,0},{6,2},{8,12},{10,14},{12,8},{14,10},{16,20},{18,... | collective-permute-start | bytes 786440 | tf_op jit(solution)/shard_map/ppermute | solution.py:19
  70.5 15.3 %collective-permute-start.16 = (f16[512,256]{1,0:T(8,128)(2,1)S(1)}, f16[512,256]{1,0:T(8,128)(2,1)S(1)}, u32[]{:S(2)}, u32[]{:S(2)}) collective-permute-start(f16[512,256]{1,0:T(8,128)(2,1)S(1)} %convert_element_type.146), channel_id=1, source_target_pairs={{0,2},{2,0},{4,6},{6,4},{8,10},{10,8},{12,14},{14,12},{16,18},{18,... | collective-permute-start | bytes 786440 | tf_op jit(solution)/shard_map/ppermute | solution.py:19
  73.1 16.9 %collective-permute-start.21 = (f16[512,256]{1,0:T(8,128)(2,1)S(1)}, f16[512,256]{1,0:T(8,128)(2,1)S(1)}, u32[]{:S(2)}, u32[]{:S(2)}) collective-permute-start(f16[512,256]{1,0:T(8,128)(2,1)S(1)} %convert_element_type.156), channel_id=1, source_target_pairs={{0,4},{2,6},{4,0},{6,2},{8,12},{10,14},{12,8},{14,10},{16,20},{18,... | collective-permute-start | bytes 786440 | tf_op jit(solution)/shard_map/ppermute | solution.py:19
  76.1 15.3 %collective-permute-start.22 = (f16[512,256]{1,0:T(8,128)(2,1)S(1)}, f16[512,256]{1,0:T(8,128)(2,1)S(1)}, u32[]{:S(2)}, u32[]{:S(2)}) collective-permute-start(f16[512,256]{1,0:T(8,128)(2,1)S(1)} %convert_element_type.158), channel_id=1, source_target_pairs={{0,2},{2,0},{4,6},{6,4},{8,10},{10,8},{12,14},{14,12},{16,18},{18,... | collective-permute-start | bytes 786440 | tf_op jit(solution)/shard_map/ppermute | solution.py:19
  78.7 16.9 %collective-permute-start.27 = (f16[512,256]{1,0:T(8,128)(2,1)S(1)}, f16[512,256]{1,0:T(8,128)(2,1)S(1)}, u32[]{:S(2)}, u32[]{:S(2)}) collective-permute-start(f16[512,256]{1,0:T(8,128)(2,1)S(1)} %convert_element_type.168), channel_id=1, source_target_pairs={{0,4},{2,6},{4,0},{6,2},{8,12},{10,14},{12,8},{14,10},{16,20},{18,... | collective-permute-start | bytes 786440 | tf_op jit(solution)/shard_map/ppermute | solution.py:19
  84.4 11.8 %collective-permute-start.28 = (f16[512,256]{1,0:T(8,128)(2,1)S(1)}, f16[512,256]{1,0:T(8,128)(2,1)S(1)}, u32[]{:S(2)}, u32[]{:S(2)}) collective-permute-start(f16[512,256]{1,0:T(8,128)(2,1)S(1)} %convert_element_type.170), channel_id=1, source_target_pairs={{0,2},{2,0},{4,6},{6,4},{8,10},{10,8},{12,14},{14,12},{16,18},{18,... | collective-permute-start | bytes 786440 | tf_op jit(solution)/shard_map/ppermute | solution.py:19
  85.8 13.9 %collective-permute-start.33 = (f16[512,256]{1,0:T(8,128)(2,1)S(1)}, f16[512,256]{1,0:T(8,128)(2,1)S(1)}, u32[]{:S(2)}, u32[]{:S(2)}) collective-permute-start(f16[512,256]{1,0:T(8,128)(2,1)S(1)} %convert_element_type.180), channel_id=1, source_target_pairs={{0,4},{2,6},{4,0},{6,2},{8,12},{10,14},{12,8},{14,10},{16,20},{18,... | collective-permute-start | bytes 786440 | tf_op jit(solution)/shard_map/ppermute | solution.py:19
  95.6 14.7 %collective-permute-start.23 = (f16[2,256,256]{2,1,0:T(8,128)(2,1)S(1)}, f16[2,256,256]{2,1,0:T(8,128)(2,1)S(1)}, u32[]{:S(2)}, u32[]{:S(2)}) collective-permute-start(f16[2,256,256]{2,1,0:T(8,128)(2,1)S(1)} %pad_maximum_fusion.5), channel_id=1, source_target_pairs={{0,8},{2,10},{4,12},{6,14},{8,0},{10,2},{12,4},{14,6},{16,24},{18,... | collective-permute-start | bytes 786440 | tf_op jit(solution)/shard_map/ppermute | solution.py:19
  96.3 21.0 %collective-permute-start.29 = (f16[2,256,256]{2,1,0:T(8,128)(2,1)S(1)}, f16[2,256,256]{2,1,0:T(8,128)(2,1)S(1)}, u32[]{:S(2)}, u32[]{:S(2)}) collective-permute-start(f16[2,256,256]{2,1,0:T(8,128)(2,1)S(1)} %pad_maximum_fusion.6), channel_id=1, source_target_pairs={{0,8},{2,10},{4,12},{6,14},{8,0},{10,2},{12,4},{14,6},{16,24},{18,... | collective-permute-start | bytes 786440 | tf_op jit(solution)/shard_map/ppermute | solution.py:19
  100.0 21.5 %collective-permute-start.35 = (f16[2,256,256]{2,1,0:T(8,128)(2,1)S(1)}, f16[2,256,256]{2,1,0:T(8,128)(2,1)S(1)}, u32[]{:S(2)}, u32[]{:S(2)}) collective-permute-start(f16[2,256,256]{2,1,0:T(8,128)(2,1)S(1)} %pad_maximum_fusion.7), channel_id=1, source_target_pairs={{0,8},{2,10},{4,12},{6,14},{8,0},{10,2},{12,4},{14,6},{16,24},{18,... | collective-permute-start | bytes 786440 | tf_op jit(solution)/shard_map/ppermute | solution.py:19
  100.5 21.1 %collective-permute-start.18 = (f16[2,128,256]{2,1,0:T(8,128)(2,1)S(1)}, f16[2,128,256]{2,1,0:T(8,128)(2,1)S(1)}, u32[]{:S(2)}, u32[]{:S(2)}) collective-permute-start(f16[2,128,256]{2,1,0:T(8,128)(2,1)S(1)} %fusion.23), channel_id=1, source_target_pairs={{0,16},{2,18},{4,20},{6,22},{8,24},{10,26},{12,28},{14,30},{16,0},... | collective-permute-start | bytes 393224 | tf_op jit(solution)/shard_map/ppermute | solution.py:19
  110.3 18.3 %collective-permute-start.24 = (f16[2,128,256]{2,1,0:T(8,128)(2,1)S(1)}, f16[2,128,256]{2,1,0:T(8,128)(2,1)S(1)}, u32[]{:S(2)}, u32[]{:S(2)}) collective-permute-start(f16[2,128,256]{2,1,0:T(8,128)(2,1)S(1)} %fusion.20), channel_id=1, source_target_pairs={{0,16},{2,18},{4,20},{6,22},{8,24},{10,26},{12,28},{14,30},{16,0},... | collective-permute-start | bytes 393224 | tf_op jit(solution)/shard_map/ppermute | solution.py:19
  117.3 14.0 %collective-permute-start.30 = (f16[2,128,256]{2,1,0:T(8,128)(2,1)S(1)}, f16[2,128,256]{2,1,0:T(8,128)(2,1)S(1)}, u32[]{:S(2)}, u32[]{:S(2)}) collective-permute-start(f16[2,128,256]{2,1,0:T(8,128)(2,1)S(1)} %fusion.17), channel_id=1, source_target_pairs={{0,16},{2,18},{4,20},{6,22},{8,24},{10,26},{12,28},{14,30},{16,0},... | collective-permute-start | bytes 393224 | tf_op jit(solution)/shard_map/ppermute | solution.py:19
  121.5 11.1 %collective-permute-start.36 = (f16[2,128,256]{2,1,0:T(8,128)(2,1)S(1)}, f16[2,128,256]{2,1,0:T(8,128)(2,1)S(1)}, u32[]{:S(2)}, u32[]{:S(2)}) collective-permute-start(f16[2,128,256]{2,1,0:T(8,128)(2,1)S(1)} %fusion.14), channel_id=1, source_target_pairs={{0,16},{2,18},{4,20},{6,22},{8,24},{10,26},{12,28},{14,30},{16,0},... | collective-permute-start | bytes 393224 | tf_op jit(solution)/shard_map/ppermute | solution.py:19
  (27 other events, 186.9 us)
